TPU v7x, 32 devices: a whole 2x2x4 slice. The times are simulated.
32 devices in a mesh: attn: 4 (over y, core), expert: 4 (over z), loop: 2 (over x).
Axes of the slice: x: 2, y: 2, z: 4, core: 2. Of those that a mesh axis runs over, the one named last changes fastest.
Arguments:
- resid: bfloat16 [64, 3072], P(('expert', 'loop', 'attn')), may hold values from -33 to 33
- query: bfloat16 [64, 3072], P(('expert', 'loop', 'attn')), may hold values from -68.75573 to 68.75573
- key_cache: bfloat16 [64, 256, 512], P(('expert', 'loop', 'attn')), may hold values from -6 to 6
- value_cache: bfloat16 [64, 256, 512], P(('expert', 'loop', 'attn')), may hold values from -6 to 6
- new_key: bfloat16 [64, 512], P(('expert', 'loop', 'attn')), may hold values from -6 to 6
- new_value: bfloat16 [64, 512], P(('expert', 'loop', 'attn')), may hold values from -6 to 6
- cache_len: int32 [64], P(('expert', 'loop', 'attn')), may hold values from 2 to 256, as said below
- norm_gain: float32 [3072], replicated, may hold values from 0.5 to 1.5
- gate_weight: bfloat16 [4, 3072, 8192], P('expert', 'attn', 'loop'), may hold values from -0.109375 to 0.109375
- up_weight: bfloat16 [4, 3072, 8192], P('expert', 'attn', 'loop'), may hold values from -0.109375 to 0.109375
- down_weight: bfloat16 [4, 8192, 3072], P('expert', 'loop', 'attn'), may hold values from -0.0625 to 0.0625
- block_rows: int32 [4, 1, 128], P('expert'), may hold values from -1 to 63, as said below
- slot_weight: float32 [4, 1, 128], P('expert'), may hold values from 0.1 to 1
Outputs:
- layer_out: bfloat16 [64, 3072], P(('expert', 'loop', 'attn'))
Inputs may be any that keep to these rules, and one draw needn't show every extreme that they name: `block_rows`: each of the 64 rows is named in the lists of exactly two different experts and nowhere else; within a list the rows ascend and fill the slots from the first one on; unused slots hold -1. One expert, drawn from the seed, is named by exactly 32 rows; the other experts by nearly equal numbers of rows. `cache_len`: some row uses all 256 positions.
All inputs are finite; a program needn't handle non-finite values.
Results may differ from a plain program's by a relative error of at most 0.0054.
Values may be sent and summed in bfloat16 or wider, within the bound.
A program may use at most 128 MiB of HBM per device.

v0:
```python
import jax
import jax.numpy as jnp
from jax import lax
from jax.sharding import PartitionSpec as P

Q_HEADS = 24
KV_HEADS = 4
HEAD = 128
CACHE = 256


def attend(query, key_cache, value_cache, new_key, new_value, cache_len):
    rows_here = query.shape[0]
    groups = Q_HEADS // KV_HEADS
    score_scale = HEAD ** (-0.5)
    queries = query.reshape(rows_here, KV_HEADS, groups, HEAD)
    cached_keys = key_cache.reshape(rows_here, CACHE, KV_HEADS, HEAD)
    cached_values = value_cache.reshape(rows_here, CACHE, KV_HEADS, HEAD)
    own_keys = new_key.reshape(rows_here, KV_HEADS, HEAD)
    own_values = new_value.reshape(rows_here, KV_HEADS, 1, HEAD)
    scores = (
        jnp.einsum("rkgd,rlkd->rkgl", queries, cached_keys, preferred_element_type=jnp.float32)
        * score_scale
    )
    own_score = (
        jnp.einsum("rkgd,rkd->rkg", queries, own_keys, preferred_element_type=jnp.float32)
        * score_scale
    )
    cache_live = jnp.arange(CACHE)[None, :] < cache_len[:, None]
    scores = jnp.where(cache_live[:, None, None, :], scores, -jnp.inf)
    row_max = jnp.maximum(jnp.max(scores, axis=-1), own_score)
    cached_exp = jnp.exp(scores - row_max[..., None])
    own_exp = jnp.exp(own_score - row_max)
    denominator = jnp.sum(cached_exp, axis=-1) + own_exp
    cached_prob = (cached_exp / denominator[..., None]).astype(jnp.bfloat16)
    own_prob = (own_exp / denominator).astype(jnp.bfloat16)
    attended = jnp.einsum(
        "rkgl,rlkd->rkgd", cached_prob, cached_values, preferred_element_type=jnp.float32
    )
    attended = attended + jnp.einsum(
        "rkg,rkxd->rkgd", own_prob, own_values, preferred_element_type=jnp.float32
    )
    return attended.reshape(rows_here, Q_HEADS * HEAD)


def per_device(
    resid,
    query,
    key_cache,
    value_cache,
    new_key,
    new_value,
    cache_len,
    norm_gain,
    gate_weight,
    up_weight,
    down_weight,
    block_rows,
    slot_weight,
):
    attended = attend(query, key_cache, value_cache, new_key, new_value, cache_len)
    residual = (resid.astype(jnp.float32) + attended).astype(jnp.bfloat16)
    residual_wide = residual.astype(jnp.float32)
    normed = (
        residual_wide
        * lax.rsqrt(jnp.mean(residual_wide * residual_wide, axis=-1, keepdims=True) + 1e-05)
        * norm_gain
    ).astype(jnp.bfloat16)
    width_parts = lax.all_to_all(normed, "attn", split_axis=1, concat_axis=0, tiled=True)
    every_row = lax.all_gather(width_parts, ("expert", "loop"), axis=0, tiled=True)
    total_rows = every_row.shape[0]
    slot_total = block_rows.shape[1] * block_rows.shape[2]
    slot_rows = block_rows.reshape(slot_total)
    slot_live = slot_rows >= 0
    picked = jnp.take(every_row, jnp.where(slot_live, slot_rows, 0), axis=0)
    picked = jnp.where(slot_live[:, None], picked, jnp.zeros_like(picked))
    gate_part = jnp.dot(picked, gate_weight[0], preferred_element_type=jnp.float32)
    up_part = jnp.dot(picked, up_weight[0], preferred_element_type=jnp.float32)
    gate_total, up_total = lax.psum((gate_part, up_part), "attn")
    hidden = (jax.nn.silu(gate_total) * up_total).astype(jnp.bfloat16)
    expert_out = jnp.dot(hidden, down_weight[0], preferred_element_type=jnp.float32)
    weighted = expert_out * jnp.where(slot_live, slot_weight.reshape(slot_total), 0.0)[:, None]
    target = jnp.where(slot_live, slot_rows, total_rows)
    dense_rows = (
        jnp.zeros((total_rows, expert_out.shape[1]), jnp.float32)
        .at[target]
        .add(weighted, mode="drop")
    )
    owned_sums = lax.psum_scatter(
        dense_rows, ("expert", "loop"), scatter_dimension=0, tiled=True
    ).astype(jnp.bfloat16)
    returned = lax.all_to_all(owned_sums, "attn", split_axis=0, concat_axis=1, tiled=True)
    return (residual.astype(jnp.float32) + returned.astype(jnp.float32)).astype(jnp.bfloat16)


def solution(mesh):
    in_specs = (
        P(("expert", "loop", "attn"), None),
        P(("expert", "loop", "attn"), None),
        P(("expert", "loop", "attn"), None, None),
        P(("expert", "loop", "attn"), None, None),
        P(("expert", "loop", "attn"), None),
        P(("expert", "loop", "attn"), None),
        P(("expert", "loop", "attn")),
        P(),
        P("expert", "attn", "loop"),
        P("expert", "attn", "loop"),
        P("expert", "loop", "attn"),
        P("expert", None, None),
        P("expert", None, None),
    )
    out_specs = P(("expert", "loop", "attn"), None)
    return jax.shard_map(
        per_device, mesh=mesh, in_specs=in_specs, out_specs=out_specs, check_vma=False
    )
```

profile of v0, /device:TPU:0, one launch (start us, length us, event | category | flops | bytes accessed | tf_op | source)
XLA Modules:
  0.0 230.8 jit_solution(8481233316567846436)
XLA Ops:
  6.5 0.0 copy-start
  6.5 0.8 reshape.133
  7.3 0.7 iota_compare_fusion
  8.1 0.7 reshape.163
  8.7 0.1 fusion.30
  8.9 0.0 copy-done
  8.9 0.3 fusion.29
  9.2 0.2 fusion.17
  9.4 0.7 reshape.142
  10.1 1.3 convolution_add_fusion
  11.4 0.8 fusion.20
  12.3 1.4 fusion.22
  13.7 4.2 %all-to-all-start = ((bf16[2,4,768]{2,0,1:T(2,128)(2,1)}), bf16[2,4,768]{2,0,1:T(2,128)(2,1)S(1)}, u32[]{:S(2)}, u32[]{:S(2)}) async-start(bf16[2,4,768]{2,0,1:T(2,128)(2,1)} %bitcast.5), calls=%async_computation | async-start | bytes 24576 | tf_op jit(solution)/shard_map/all_to_all | solution.py:69
  17.9 0.0 all-reduce.3.cloned.1.call-start
  17.9 0.7 fusion.27
  18.6 0.7 bitcast_compare_fusion
  19.2 2.5 %all-to-all-done = bf16[2,4,768]{2,0,1:T(2,128)(2,1)S(1)} async-done(((bf16[2,4,768]{2,0,1:T(2,128)(2,1)}), bf16[2,4,768]{2,0,1:T(2,128)(2,1)S(1)}, u32[]{:S(2)}, u32[]{:S(2)}) %all-to-all-start) | async-done | bytes 12320 | tf_op jit(solution)/shard_map/all_to_all | solution.py:69
  21.8 31.3 %all_gather.3 = bf16[64,768]{1,0:T(8,128)(2,1)S(1)} all-gather(bf16[8,768]{1,0:T(8,128)(2,1)S(1)} %all_to_all.27), channel_id=1, replica_groups=mesh['attn'=4,'expert'=4,'loop'=2] {'expert','loop'}, dimensions={0}, use_global_device_ids=true | all-gather | bytes 110592 | tf_op jit(solution)/shard_map/all_gather | solution.py:70
  53.1 0.0 slice-start
  53.1 0.9 gather_fusion
  53.9 0.0 slice-start.1
  54.0 5.3 %fusion.2 = f32[128,4096]{1,0:T(8,128)} fusion(bf16[1,768,4096]{2,1,0:T(8,128)(2,1)} %param.22, bf16[128,768]{1,0:T(8,128)(2,1)S(1)} %gather_fusion, pred[128]{0:T(512)(128)(4,1)S(1)} %get-tuple-element.12, pred[128]{0:T(512)(128)(4,1)S(1)} %get-tuple-element.11), kind=kOutput, calls=%fused_computation.4 | convolution fusion | flops 805502976 | bytes 8585472 | tf_op jit(solution)/shard_map/dot_general | solution.py:78
  59.3 0.0 slice-done
  59.3 0.0 slice-done.1
  59.3 2.4 %fusion.4 = f32[128,4096]{1,0:T(8,128)} fusion(bf16[1,768,4096]{2,1,0:T(8,128)(2,1)S(1)} %bitcast.56, bf16[128,768]{1,0:T(8,128)(2,1)S(1)} %gather_fusion, pred[128]{0:T(512)(128)(4,1)S(1)} %get-tuple-element.12, pred[128]{0:T(512)(128)(4,1)S(1)} %get-tuple-element.11), kind=kOutput, calls=%fused_computation.6 | convolution fusion | flops 805502976 | bytes 8585472 | tf_op jit(solution)/shard_map/dot_general | solution.py:77
  61.7 0.0 copy-start.1
  61.7 0.0 copy-start.2
  61.7 0.0 all-reduce.3.cloned.1.call-update
  61.7 0.0 reduce-scatter.2.cloned.1.call-start
  61.7 0.6 copy-done.1
  62.3 0.0 copy-done.2
  62.3 85.1 %all-reduce.3.cloned.1.call-done = (f32[128,4096]{1,0:T(8,128)}, f32[128,4096]{1,0:T(8,128)}) async-done(((f32[128,4096]{1,0:T(8,128)}, f32[128,4096]{1,0:T(8,128)}), (f32[128,4096]{1,0:T(8,128)}, f32[128,4096]{1,0:T(8,128)})) %all-reduce.3.cloned.1.call-update) | async-done | bytes 4194320 | tf_op jit(solution)/shard_map/psum | solution.py:79
  147.5 5.3 %fusion.6 = f32[128,768]{1,0:T(8,128)S(1)} fusion(bf16[1,4096,768]{2,1,0:T(8,128)(2,1)} %param.23, f32[128,4096]{1,0:T(8,128)} %get-tuple-element.5, f32[128,4096]{1,0:T(8,128)} %get-tuple-element.6, f32[128]{0:T(128)S(1)} %bitcast_select_fusion), kind=kOutput, calls=%fused_computation.9 | convolution fusion | flops 808550400 | bytes 10879488 | tf_op jit(solution)/shard_map/dot_general | solution.py:81
  152.8 2.0 scatter_custom_fusion
  154.8 0.0 reduce-scatter.2.cloned.1.call-update
  154.9 61.3 %reduce-scatter.2.cloned.1.call-done = f32[8,768]{1,0:T(8,128)} async-done(((f32[64,768]{1,0:T(8,128)}), f32[8,768]{1,0:T(8,128)}) %reduce-scatter.2.cloned.1.call-update) | async-done | bytes 24592 | tf_op jit(solution)/shard_map/reduce_scatter | solution.py:89
  216.2 0.7 convert_element_type.45
  217.0 6.4 %all_to_all.32 = bf16[4,2,768]{2,1,0:T(2,128)(2,1)S(1)} all-to-all(bf16[4,2,768]{2,1,0:T(2,128)(2,1)S(1)} %all_to_all.28), channel_id=1, replica_groups=mesh['attn'=4,'expert'=4,'loop'=2] {'attn'}, dimensions={0} | all-to-all | bytes 24576 | tf_op jit(solution)/shard_map/all_to_all | solution.py:92
  223.3 0.6 fusion.23
  (10 shorter events, 0.1 us)
Async XLA Ops:
  6.5 2.3 %copy-start = (bf16[2,256,512]{2,1,0:T(8,128)(2,1)S(1)}, bf16[2,256,512]{2,1,0:T(8,128)(2,1)}, u32[]{:S(2)}) copy-start(bf16[2,256,512]{2,1,0:T(8,128)(2,1)} %param.15) | copy-start | bytes 1572868
  13.7 8.1 %all-to-all-start = ((bf16[2,4,768]{2,0,1:T(2,128)(2,1)}), bf16[2,4,768]{2,0,1:T(2,128)(2,1)S(1)}, u32[]{:S(2)}, u32[]{:S(2)}) async-start(bf16[2,4,768]{2,0,1:T(2,128)(2,1)} %bitcast.5), calls=%async_computation | async-start | bytes 24576 | tf_op jit(solution)/shard_map/all_to_all | solution.py:69
  17.9 129.6 %all-reduce.3.cloned.1.call-start = ((), (), s32[]{:S(2)}) async-start(), calls=%async_computation.4 | async-start | bytes 8388608 | tf_op jit(solution)/shard_map/psum | solution.py:79
  53.1 6.2 %slice-start = ((s8[6291456]{0:T(1024)(128)(4,1)}), s8[2097152]{0:T(1024)(128)(4,1)S(1)}, s32[]{:S(2)}) async-start(s8[6291456]{0:T(1024)(128)(4,1)} %bitcast.55), calls=%async_computation.5 | async-start | bytes 4194304
  53.9 5.3 %slice-start.1 = ((s8[6291456]{0:T(1024)(128)(4,1)}), s8[4194304]{0:T(1024)(128)(4,1)S(1)}, s32[]{:S(2)}) async-start(s8[6291456]{0:T(1024)(128)(4,1)} %bitcast.55), calls=%async_computation.6 | async-start | bytes 8388608
  61.7 0.7 copy-start.1
  61.7 0.7 copy-start.2
  61.7 154.5 %reduce-scatter.2.cloned.1.call-start = ((), (), s32[]{:S(2)}) async-start(), calls=%async_computation.3 | async-start | bytes 221184 | tf_op jit(solution)/shard_map/reduce_scatter | solution.py:89
Sparse Core Ops, SparseCore 0:
  61.8 85.6 all-reduce.2
  155.0 61.1 reduce-scatter.1
where the time goes:
time: 231 us
  waiting for transfers between devices  149 us (65%)
  blocking collectives  37.7 us (16%)
  matrix products  14.7 us (6%)
  between operations  13.5 us (6%)
  other arithmetic  7.93 us (3%)
  starting transfers between devices  4.28 us (2%)
  local copies, waits for them, and re-layouts  3.7 us (2%)
    psum x1, waiting for transfers between devices, per_device(): gate_total, up_total = lax.psum((gate_part, up_part), 'attn')  85.1 us
    reduce_scatter x1, waiting for transfers between devices, per_device(): lax.psum_scatter(dense_rows, ('expert', 'loop'), scatter_dimension=0, til...  61.3 us
    all_gather x1, blocking collectives, per_device(): lax.all_gather(width_parts, ('expert', 'loop'), axis=0, tiled=True)  31.3 us
    all_to_all x1, blocking collectives, per_device(): lax.all_to_all(owned_sums, 'attn', split_axis=0, concat_axis=1, tiled=True)  6.36 us
    dot_general x1, matrix products, per_device(): jnp.dot(hidden, down_weight[0], preferred_element_type=jnp.float32)  5.31 us
    dot_general x1, matrix products, per_device(): up_part = jnp.dot(picked, up_weight[0], preferred_element_type=jnp.float32)  5.31 us
  transfers between devices with their start and end apart: 3, of which 3 were waited for; matrix products, arithmetic and copies ran while one was open for 1% of the time, Pallas kernels for 0%

commit v1 on v0

v1 whole, which is shorter than its diff:
```python
import functools

import jax
import jax.numpy as jnp
from jax import lax
from jax.experimental import pallas as pl
from jax.experimental.pallas import tpu as pltpu
from jax.sharding import PartitionSpec as P

Q_HEADS = 24
KV_HEADS = 4
HEAD = 128
MESH = pl.DeviceIdType.MESH
F32 = jnp.float32
BF16 = jnp.bfloat16


def kernel(
    sizes,
    len_ref,
    resid_ref,
    query_ref,
    nk_ref,
    nv_ref,
    gain_ref,
    list_ref,
    slotw_ref,
    kc_hbm,
    vc_hbm,
    wg_hbm,
    wu_hbm,
    wd_hbm,
    out_ref,
    kc,
    vc,
    wg,
    wu,
    wd,
    nb,
    xr,
    x32,
    ps,
    pr,
    cs,
    cr,
    hid,
    d32,
    ys,
    yr,
    kv_sem,
    w_sem,
    d_sem,
    x_send,
    x_recv,
    p_send,
    p_recv,
    c_send,
    c_recv,
    h_send,
    h_recv,
    f_send,
    f_recv,
    y_send,
    y_recv,
):
    n, experts, loops, cap = sizes
    total = n * experts * loops
    chips = n // 2
    here, width = resid_ref.shape
    cache = kc.shape[1]
    part = width // n
    quarter = wg.shape[2]
    rows = total * here
    slots = list_ref.shape[1]
    me_a = lax.axis_index("attn")
    me_e = lax.axis_index("expert")
    me_l = lax.axis_index("loop")
    me = (me_e * loops + me_l) * n + me_a
    core = lax.rem(me_a, 2)
    chip = lax.div(me_a, 2)
    partner = {"attn": chip * 2 + 1 - core, "expert": me_e, "loop": me_l}

    def place(index):
        group = lax.div(index, n)
        return {
            "attn": lax.rem(index, n),
            "expert": lax.div(group, loops),
            "loop": lax.rem(group, loops),
        }

    def side_of(shift, side):
        at = lax.rem(chip + shift + chips, chips)
        return at * 2 + (core if side else 1 - core)

    kv_copies = []
    for r in range(here):
        kv_copies.append(pltpu.make_async_copy(kc_hbm.at[r], kc.at[r], kv_sem.at[0, r]))
        kv_copies.append(pltpu.make_async_copy(vc_hbm.at[r], vc.at[r], kv_sem.at[1, r]))
    for copy in kv_copies:
        copy.start()

    barrier = pltpu.get_barrier_semaphore()

    def greet(d, carry):
        pl.semaphore_signal(
            barrier, inc=1, device_id=place(lax.rem(me + d, total)), device_id_type=MESH
        )
        return carry

    lax.fori_loop(1, total, greet, 0)

    shifts = list(range(1, chips)) + [0]
    w_copies = []
    for i, shift in enumerate(shifts):
        for side in range(2):
            k = 2 * i + side
            col = pl.multiple_of(side_of(shift, side) * quarter, quarter)
            pair = (
                pltpu.make_async_copy(wg_hbm.at[0, :, pl.ds(col, quarter)], wg.at[k], w_sem.at[0, k]),
                pltpu.make_async_copy(wu_hbm.at[0, :, pl.ds(col, quarter)], wu.at[k], w_sem.at[1, k]),
            )
            for copy in pair:
                copy.start()
            w_copies.append(pair)
    d_copies = []
    for shift in range(chips):
        for j in range(2):
            k = 2 * shift + j
            row = pl.multiple_of(side_of(-shift, 1 - j) * quarter, quarter)
            copy = pltpu.make_async_copy(wd_hbm.at[0, pl.ds(row, quarter), :], wd.at[k], d_sem.at[k])
            copy.start()
            d_copies.append(copy)

    rows_pad = max(rows, 128)
    slot_rows = list_ref[...]
    hot_t = jnp.where(
        lax.broadcasted_iota(jnp.int32, (rows_pad, slots), 0) == slot_rows, 1.0, 0.0
    ).astype(F32)
    hot = hot_t.T[:cap, :rows].astype(BF16)
    hot_t = hot_t[:rows]
    row_weight = jnp.sum(hot_t * slotw_ref[...], axis=1, keepdims=True)
    hot_t = hot_t.astype(BF16)

    groups = Q_HEADS // KV_HEADS
    scale = HEAD ** (-0.5)
    head_of = lax.broadcasted_iota(jnp.int32, (Q_HEADS, HEAD), 0) // groups
    position = lax.broadcasted_iota(jnp.int32, (Q_HEADS, cache), 1)
    queries = query_ref[...].astype(F32)
    new_keys = nk_ref[...].astype(F32)
    new_values = nv_ref[...].astype(F32)
    attended_rows = []
    for r in range(here):
        q24 = jnp.concatenate(
            [queries[r : r + 1, j * HEAD : (j + 1) * HEAD] for j in range(Q_HEADS)], axis=0
        )
        own_key = jnp.zeros((Q_HEADS, HEAD), F32)
        own_value = jnp.zeros((Q_HEADS, HEAD), F32)
        for g in range(KV_HEADS):
            lanes = slice(g * HEAD, (g + 1) * HEAD)
            own_key = jnp.where(head_of == g, new_keys[r : r + 1, lanes], own_key)
            own_value = jnp.where(head_of == g, new_values[r : r + 1, lanes], own_value)
        q_wide = jnp.concatenate(
            [jnp.where(head_of == g, q24, 0.0) for g in range(KV_HEADS)], axis=1
        ).astype(BF16)
        own_score = jnp.sum(q24 * own_key, axis=1, keepdims=True) * scale
        kv_copies[2 * r].wait()
        scores = (
            lax.dot_general(
                q_wide, kc[r], (((1,), (1,)), ((), ())), preferred_element_type=F32
            )
            * scale
        )
        scores = jnp.where(position < len_ref[r], scores, -jnp.inf)
        top = jnp.maximum(jnp.max(scores, axis=1, keepdims=True), own_score)
        exps = jnp.exp(scores - top)
        own_exp = jnp.exp(own_score - top)
        denominator = jnp.sum(exps, axis=1, keepdims=True) + own_exp
        probs = (exps / denominator).astype(BF16)
        own_prob = (own_exp / denominator).astype(BF16).astype(F32)
        kv_copies[2 * r + 1].wait()
        mixed = jnp.dot(probs, vc[r], preferred_element_type=F32)
        attended = own_prob * own_value
        for g in range(KV_HEADS):
            attended = attended + jnp.where(
                head_of == g, mixed[:, g * HEAD : (g + 1) * HEAD], 0.0
            )
        attended_rows.append(
            jnp.concatenate([attended[j : j + 1, :] for j in range(Q_HEADS)], axis=1)
        )
    attended = jnp.concatenate(attended_rows, axis=0)
    residual = (resid_ref[...].astype(F32) + attended).astype(BF16).astype(F32)
    normed = (
        residual
        * lax.rsqrt(jnp.mean(residual * residual, axis=-1, keepdims=True) + 1e-05)
        * gain_ref[...]
    ).astype(BF16)
    for a in range(n):
        nb[a] = normed[:, a * part : (a + 1) * part]

    pl.semaphore_wait(barrier, total - 1)

    def send_x(d, carry):
        to = lax.rem(me + d, total)
        pltpu.make_async_remote_copy(
            src_ref=nb.at[lax.rem(to, n)],
            dst_ref=xr.at[me],
            send_sem=x_send,
            recv_sem=x_recv,
            device_id=place(to),
            device_id_type=MESH,
        ).start()
        return carry

    lax.fori_loop(1, total, send_x, 0)
    xr[me] = nb[me_a]

    def wait_all(buffer, sem):
        block = buffer.at[pl.ds(0, total - 1)]
        pltpu.make_async_copy(block, block, sem).wait()

    wait_all(xr, x_recv)
    tiles = x32.shape[0]
    per_tile = x32.shape[1] // here

    def unpack(t, carry):
        for j in range(per_tile):
            x32[t, j * here : (j + 1) * here, :] = xr[t * per_tile + j].astype(F32)
        return carry

    lax.fori_loop(0, tiles, unpack, 0, unroll=min(8, tiles))
    every_row = x32[...].reshape(rows, part).astype(BF16)
    picked = jnp.dot(hot, every_row, preferred_element_type=F32).astype(BF16)

    def gate_up(k):
        for copy in w_copies[k]:
            copy.wait()
        gate = jnp.dot(picked, wg[k], preferred_element_type=F32)
        up = jnp.dot(picked, wu[k], preferred_element_type=F32)
        return jnp.concatenate([gate, up], axis=0)

    sends = []
    own = None
    for i, shift in enumerate(shifts):
        ps[i] = gate_up(2 * i).astype(BF16)
        to_partner = pltpu.make_async_remote_copy(
            src_ref=ps.at[i],
            dst_ref=pr.at[i],
            send_sem=p_send.at[i],
            recv_sem=p_recv.at[i],
            device_id=partner,
            device_id_type=MESH,
        )
        to_partner.start()
        sends.append(to_partner)
        own = gate_up(2 * i + 1)
        to_partner.wait_recv()
        own = own + pr[i].astype(F32)
        if shift:
            cs[shift - 1] = own.astype(BF16)
            across = pltpu.make_async_remote_copy(
                src_ref=cs.at[shift - 1],
                dst_ref=cr.at[shift - 1],
                send_sem=c_send.at[shift - 1],
                recv_sem=c_recv.at[shift - 1],
                device_id={"attn": side_of(shift, 1), "expert": me_e, "loop": me_l},
                device_id_type=MESH,
            )
            across.start()
            sends.append(across)
    for shift in range(1, chips):
        sends[2 * shift - 1].wait_recv()
        own = own + cr[shift - 1].astype(F32)
    gate = own[:cap]
    hid[0] = (gate / (1.0 + jnp.exp(-gate)) * own[cap:]).astype(BF16)

    across_h = []
    for shift in range(1, chips):
        copy = pltpu.make_async_remote_copy(
            src_ref=hid.at[0],
            dst_ref=hid.at[2 * shift],
            send_sem=h_send.at[shift],
            recv_sem=h_recv.at[shift],
            device_id={"attn": side_of(shift, 1), "expert": me_e, "loop": me_l},
            device_id_type=MESH,
        )
        copy.start()
        across_h.append(copy)

    def forward(shift):
        copy = pltpu.make_async_remote_copy(
            src_ref=hid.at[2 * shift],
            dst_ref=hid.at[2 * shift + 1],
            send_sem=f_send.at[shift],
            recv_sem=f_recv.at[shift],
            device_id=partner,
            device_id_type=MESH,
        )
        copy.start()
        return copy

    def down(k):
        d_copies[k].wait()
        return jnp.dot(hid[k], wd[k], preferred_element_type=F32)

    near = forward(0)
    expert_out = down(0)
    near.wait_recv()
    expert_out = expert_out + down(1)
    sends.append(near)
    for shift in range(1, chips):
        across_h[shift - 1].wait_recv()
        near = forward(shift)
        expert_out = expert_out + down(2 * shift)
        near.wait_recv()
        expert_out = expert_out + down(2 * shift + 1)
        sends.append(near)

    if slots > cap:
        expert_out = jnp.concatenate([expert_out, jnp.zeros((slots - cap, part), F32)], axis=0)
    high = expert_out.astype(BF16)
    low = (expert_out - high.astype(F32)).astype(BF16)
    dense = (
        jnp.dot(hot_t, high, preferred_element_type=F32)
        + jnp.dot(hot_t, low, preferred_element_type=F32)
    ) * row_weight
    d32[...] = dense.reshape(d32.shape)

    def pack(t, carry):
        for j in range(per_tile):
            ys[t * per_tile + j] = d32[t, j * here : (j + 1) * here, :].astype(BF16)
        return carry

    lax.fori_loop(0, tiles, pack, 0, unroll=min(8, tiles))

    def send_y(d, carry):
        to = lax.rem(me + d, total)
        pltpu.make_async_remote_copy(
            src_ref=ys.at[to],
            dst_ref=yr.at[me],
            send_sem=y_send,
            recv_sem=y_recv,
            device_id=place(to),
            device_id_type=MESH,
        ).start()
        return carry

    lax.fori_loop(1, total, send_y, 0)
    yr[me] = ys[me]
    wait_all(yr, y_recv)
    sources = total // n

    def add(g, sums):
        return tuple(sums[a] + yr[g * n + a].astype(F32) for a in range(n))

    sums = lax.fori_loop(
        0,
        sources,
        add,
        tuple(jnp.zeros((here, part), F32) for _ in range(n)),
        unroll=min(8, sources),
    )
    moe = jnp.concatenate(sums, axis=1).astype(BF16).astype(F32)
    out_ref[...] = (residual + moe).astype(BF16)

    for copy in sends + across_h:
        copy.wait_send()
    wait_all(xr, x_send)
    wait_all(yr, y_send)


def per_device(
    n,
    experts,
    loops,
    resid,
    query,
    key_cache,
    value_cache,
    new_key,
    new_value,
    cache_len,
    norm_gain,
    gate_weight,
    up_weight,
    down_weight,
    block_rows,
    slot_weight,
):
    here, width = resid.shape
    total = n * experts * loops
    chips = n // 2
    rows = here * total
    part = width // n
    quarter = gate_weight.shape[2] // n
    slots = block_rows.shape[1] * block_rows.shape[2]
    busiest = rows // 2
    shared = -(-(2 * rows - busiest) // (experts - 1))
    cap = min(slots, rows, (max(busiest, shared) // 8 + 1) * 8)
    cache, kv_width = key_cache.shape[1:]
    dma = pltpu.SemaphoreType.DMA
    vmem = pl.BlockSpec(memory_space=pltpu.VMEM)
    hbm = pl.BlockSpec(memory_space=pl.ANY)
    scratch = [
        pltpu.VMEM((here, cache, kv_width), BF16),
        pltpu.VMEM((here, cache, kv_width), BF16),
        pltpu.VMEM((n, part, quarter), BF16),
        pltpu.VMEM((n, part, quarter), BF16),
        pltpu.VMEM((n, quarter, part), BF16),
        pltpu.VMEM((n, here, part), BF16),
        pltpu.VMEM((total, here, part), BF16),
        pltpu.VMEM((rows // 8, 8, part), F32),
        pltpu.VMEM((chips, 2 * cap, quarter), BF16),
        pltpu.VMEM((chips, 2 * cap, quarter), BF16),
        pltpu.VMEM((chips - 1, 2 * cap, quarter), BF16),
        pltpu.VMEM((chips - 1, 2 * cap, quarter), BF16),
        pltpu.VMEM((n, cap, quarter), BF16),
        pltpu.VMEM((rows // 8, 8, part), F32),
        pltpu.VMEM((total, here, part), BF16),
        pltpu.VMEM((total, here, part), BF16),
        dma((2, here)),
        dma((2, n)),
        dma((n,)),
        dma,
        dma,
        dma((chips,)),
        dma((chips,)),
        dma((chips - 1,)),
        dma((chips - 1,)),
        dma((chips,)),
        dma((chips,)),
        dma((chips,)),
        dma((chips,)),
        dma,
        dma,
    ]
    return pl.pallas_call(
        functools.partial(kernel, (n, experts, loops, cap)),
        out_shape=jax.ShapeDtypeStruct((here, width), BF16),
        in_specs=[pl.BlockSpec(memory_space=pltpu.SMEM)] + [vmem] * 7 + [hbm] * 5,
        out_specs=vmem,
        scratch_shapes=scratch,
        compiler_params=pltpu.CompilerParams(
            collective_id=0, has_side_effects=True, vmem_limit_bytes=56 << 20
        ),
        name="moe_decode",
    )(
        cache_len,
        resid,
        query,
        new_key,
        new_value,
        norm_gain.reshape(1, width),
        block_rows.reshape(1, slots),
        slot_weight.reshape(1, slots),
        key_cache,
        value_cache,
        gate_weight,
        up_weight,
        down_weight,
    )


def solution(mesh):
    in_specs = (
        P(("expert", "loop", "attn"), None),
        P(("expert", "loop", "attn"), None),
        P(("expert", "loop", "attn"), None, None),
        P(("expert", "loop", "attn"), None, None),
        P(("expert", "loop", "attn"), None),
        P(("expert", "loop", "attn"), None),
        P(("expert", "loop", "attn")),
        P(),
        P("expert", "attn", "loop"),
        P("expert", "attn", "loop"),
        P("expert", "loop", "attn"),
        P("expert", None, None),
        P("expert", None, None),
    )
    out_specs = P(("expert", "loop", "attn"), None)
    body = functools.partial(
        per_device, mesh.shape["attn"], mesh.shape["expert"], mesh.shape["loop"]
    )
    return jax.shard_map(body, mesh=mesh, in_specs=in_specs, out_specs=out_specs, check_vma=False)
```

time: 231 us -> 32.6 us (0.14)
  waiting for transfers between devices: 149 us -> 0 us
  blocking collectives: 37.7 us -> 0 us
  Pallas kernels: 0 us -> 31 us
  matrix products: 14.7 us -> 0 us
  between operations: 13.5 us -> 0.01 us
  other arithmetic: 7.93 us -> 0 us
  starting transfers between devices: 4.28 us -> 0 us
  local copies, waits for them, and re-layouts: 3.7 us -> 1.32 us
    psum x1 -> x0, waiting for transfers between devices: 85.1 us -> none  [per_device(): gate_total, up_total = lax.psum((gate_part, up_part), 'attn')]
    reduce_scatter x1 -> x0, waiting for transfers between devices: 61.3 us -> none  [per_device(): lax.psum_scatter(dense_rows, ('expert', 'loop'), scatter_dimension=0, til...]
    all_gather x1 -> x0, blocking collectives: 31.3 us -> none  [per_device(): lax.all_gather(width_parts, ('expert', 'loop'), axis=0, tiled=True)]
    pallas_call x0 -> x1, Pallas kernels: none -> 31 us  [per_device(): pl.pallas_call(functools.partial(kernel, (n, experts, loops, cap)), out_s...]
    dot_general x6 -> x0, matrix products: 14.7 us -> none  [the longest x1 5.31 us: per_device(): jnp.dot(hidden, down_weight[0], preferred_element_type=jnp.float32)]
    all_to_all x1 -> x0, blocking collectives: 6.36 us -> none  [per_device(): lax.all_to_all(owned_sums, 'attn', split_axis=0, concat_axis=1, tiled=True)]
    all_to_all x1 -> x0, starting transfers between devices: 4.24 us -> none  [per_device(): lax.all_to_all(normed, 'attn', split_axis=1, concat_axis=0, tiled=True)]
    convert_element_type x4 -> x0, other arithmetic: 2.76 us -> none  [the longest x1 1.39 us: per_device(): normed = (residual_wide * lax.rsqrt(jnp.mean(residual_wide * residual_wid...]
  transfers between devices with their start and end apart: 3 -> 0, of which waited for: 3 -> 0; matrix products, arithmetic and copies ran while one was open for 1% -> 0% of each run, Pallas kernels for 0% -> 0%
where the time goes in v1:
time: 32.6 us; the launch traced here: 32.3 us
  Pallas kernels  31 us (95%)
  local copies, waits for them, and re-layouts  1.32 us (4%)
    pallas_call x1, Pallas kernels, per_device(): pl.pallas_call(functools.partial(kernel, (n, experts, loops, cap)), out_s...  31 us
    unnamed x1, local copies, waits for them, and re-layouts  1.32 us

profile of v1, /device:TPU:0, one launch (start us, length us, event | category | flops | bytes accessed | tf_op | source)
XLA Modules:
  0.0 32.3 jit_solution(15265432466045764693)
XLA Ops:
  0.0 31.0 %moe_decode.1 = bf16[2,3072]{1,0:T(2,128)(2,1)} custom-call(s32[2]{0:T(128)} %len_ref.1, bf16[2,3072]{1,0:T(2,128)(2,1)} %resid_ref.1, bf16[2,3072]{1,0:T(2,128)(2,1)} %query_ref.1, bf16[2,512]{1,0:T(2,128)(2,1)} %nk_ref.1, bf16[2,512]{1,0:T(2,128)(2,1)} %nv_ref.1, f32[1,3072]{1,0:T(1,128)} %bitcast.3, s32[1,128]{1,0:T(1,128)} %bitcast.4, f32[1,128]{1,0:T(1,128)} %bitcast.5, ...), custom_call_target="tpu_custom_call" | custom-call | tf_op jit(solution)/shard_map/moe_decode/pallas_call | solution.py:436
  31.0 1.3 %copy.15 = bf16[2,3072]{1,0:T(2,128)(2,1)} copy(bf16[2,3072]{1,0:T(2,128)(2,1)} %moe_decode.1) | data formatting | bytes 24576

commit v2 on v1

--- a/solution.py
+++ b/solution.py
@@ -13,6 +13,7 @@
 MESH = pl.DeviceIdType.MESH
 F32 = jnp.float32
 BF16 = jnp.bfloat16
+CUTS = 2
 
 
 def kernel(
@@ -41,6 +42,7 @@
     x32,
     ps,
     pr,
+    own,
     cs,
     cr,
     hid,
@@ -63,13 +65,14 @@
     y_send,
     y_recv,
 ):
-    n, experts, loops, cap = sizes
+    n, experts, loops, cap, cuts = sizes
     total = n * experts * loops
     chips = n // 2
     here, width = resid_ref.shape
     cache = kc.shape[1]
     part = width // n
-    quarter = wg.shape[2]
+    piece = wg.shape[2]
+    quarter = piece * cuts
     rows = total * here
     slots = list_ref.shape[1]
     me_a = lax.axis_index("attn")
@@ -80,13 +83,28 @@
     chip = lax.div(me_a, 2)
     partner = {"attn": chip * 2 + 1 - core, "expert": me_e, "loop": me_l}
 
-    def place(index):
-        group = lax.div(index, n)
-        return {
-            "attn": lax.rem(index, n),
-            "expert": lax.div(group, loops),
-            "loop": lax.rem(group, loops),
-        }
+    sources = total // n
+    group = me_e * loops + me_l
+    lanes_of = [lax.rem(me_a + d, n) for d in range(n)]
+
+    def peers_of(d, first, act):
+        other = lax.rem(group + d, sources)
+        expert = lax.div(other, loops)
+        loop = lax.rem(other, loops)
+        for k in range(first, n):
+            act(
+                other * n + lanes_of[k],
+                lanes_of[k],
+                {"attn": lanes_of[k], "expert": expert, "loop": loop},
+            )
+
+    def each_peer(act):
+        def step(d, carry):
+            peers_of(d, 0, act)
+            return carry
+
+        lax.fori_loop(1, sources, step, 0, unroll=sources <= 8)
+        peers_of(0, 1, act)
 
     def side_of(shift, side):
         at = lax.rem(chip + shift + chips, chips)
@@ -101,35 +119,40 @@
 
     barrier = pltpu.get_barrier_semaphore()
 
-    def greet(d, carry):
-        pl.semaphore_signal(
-            barrier, inc=1, device_id=place(lax.rem(me + d, total)), device_id_type=MESH
-        )
-        return carry
-
-    lax.fori_loop(1, total, greet, 0)
+    def greet(index, lane, device):
+        pl.semaphore_signal(barrier, inc=1, device_id=device, device_id_type=MESH)
+
+    each_peer(greet)
 
     shifts = list(range(1, chips)) + [0]
-    w_copies = []
-    for i, shift in enumerate(shifts):
+    w_copies = {}
+    for shift in shifts:
         for side in range(2):
-            k = 2 * i + side
-            col = pl.multiple_of(side_of(shift, side) * quarter, quarter)
-            pair = (
-                pltpu.make_async_copy(wg_hbm.at[0, :, pl.ds(col, quarter)], wg.at[k], w_sem.at[0, k]),
-                pltpu.make_async_copy(wu_hbm.at[0, :, pl.ds(col, quarter)], wu.at[k], w_sem.at[1, k]),
-            )
-            for copy in pair:
-                copy.start()
-            w_copies.append(pair)
+            for cut in range(cuts):
+                k = len(w_copies)
+                col = pl.multiple_of(side_of(shift, side) * quarter + cut * piece, piece)
+                pair = (
+                    pltpu.make_async_copy(
+                        wg_hbm.at[0, :, pl.ds(col, piece)], wg.at[k], w_sem.at[0, k]
+                    ),
+                    pltpu.make_async_copy(
+                        wu_hbm.at[0, :, pl.ds(col, piece)], wu.at[k], w_sem.at[1, k]
+                    ),
+                )
+                for copy in pair:
+                    copy.start()
+                w_copies[shift, side, cut] = (k, pair)
     d_copies = []
     for shift in range(chips):
         for j in range(2):
-            k = 2 * shift + j
-            row = pl.multiple_of(side_of(-shift, 1 - j) * quarter, quarter)
-            copy = pltpu.make_async_copy(wd_hbm.at[0, pl.ds(row, quarter), :], wd.at[k], d_sem.at[k])
-            copy.start()
-            d_copies.append(copy)
+            for cut in range(cuts):
+                k = (2 * shift + j) * cuts + cut
+                row = pl.multiple_of(side_of(-shift, 1 - j) * quarter + cut * piece, piece)
+                copy = pltpu.make_async_copy(
+                    wd_hbm.at[0, pl.ds(row, piece), :], wd.at[k], d_sem.at[k]
+                )
+                copy.start()
+                d_copies.append(copy)
 
     rows_pad = max(rows, 128)
     slot_rows = list_ref[...]
@@ -199,19 +222,17 @@
 
     pl.semaphore_wait(barrier, total - 1)
 
-    def send_x(d, carry):
-        to = lax.rem(me + d, total)
+    def send_x(index, lane, device):
         pltpu.make_async_remote_copy(
-            src_ref=nb.at[lax.rem(to, n)],
+            src_ref=nb.at[lane],
             dst_ref=xr.at[me],
             send_sem=x_send,
             recv_sem=x_recv,
-            device_id=place(to),
+            device_id=device,
             device_id_type=MESH,
         ).start()
-        return carry
-
-    lax.fori_loop(1, total, send_x, 0)
+
+    each_peer(send_x)
     xr[me] = nb[me_a]
 
     def wait_all(buffer, sem):
@@ -231,89 +252,93 @@
     every_row = x32[...].reshape(rows, part).astype(BF16)
     picked = jnp.dot(hot, every_row, preferred_element_type=F32).astype(BF16)
 
-    def gate_up(k):
-        for copy in w_copies[k]:
+    sends = []
+
+    def push(src_ref, dst_ref, send_sem, recv_sem, device):
+        copy = pltpu.make_async_remote_copy(
+            src_ref=src_ref,
+            dst_ref=dst_ref,
+            send_sem=send_sem,
+            recv_sem=recv_sem,
+            device_id=device,
+            device_id_type=MESH,
+        )
+        copy.start()
+        sends.append(copy)
+        return copy
+
+    def across(shift):
+        return {"attn": side_of(shift, 1), "expert": me_e, "loop": me_l}
+
+    def gate_up(shift, side, cut):
+        k, pair = w_copies[shift, side, cut]
+        for copy in pair:
             copy.wait()
         gate = jnp.dot(picked, wg[k], preferred_element_type=F32)
         up = jnp.dot(picked, wu[k], preferred_element_type=F32)
         return jnp.concatenate([gate, up], axis=0)
 
-    sends = []
-    own = None
-    for i, shift in enumerate(shifts):
-        ps[i] = gate_up(2 * i).astype(BF16)
-        to_partner = pltpu.make_async_remote_copy(
-            src_ref=ps.at[i],
-            dst_ref=pr.at[i],
-            send_sem=p_send.at[i],
-            recv_sem=p_recv.at[i],
-            device_id=partner,
-            device_id_type=MESH,
-        )
-        to_partner.start()
-        sends.append(to_partner)
-        own = gate_up(2 * i + 1)
-        to_partner.wait_recv()
-        own = own + pr[i].astype(F32)
-        if shift:
-            cs[shift - 1] = own.astype(BF16)
-            across = pltpu.make_async_remote_copy(
-                src_ref=cs.at[shift - 1],
-                dst_ref=cr.at[shift - 1],
-                send_sem=c_send.at[shift - 1],
-                recv_sem=c_recv.at[shift - 1],
-                device_id={"attn": side_of(shift, 1), "expert": me_e, "loop": me_l},
-                device_id_type=MESH,
+    def to_partner(shift):
+        copies = []
+        for cut in range(cuts):
+            k = shift * cuts + cut
+            ps[k] = gate_up(shift, 0, cut).astype(BF16)
+            copies.append(push(ps.at[k], pr.at[k], p_send.at[k], p_recv.at[k], partner))
+        return copies
+
+    crossing = {}
+    for shift in range(1, chips):
+        near = to_partner(shift)
+        for cut in range(cuts):
+            k = (shift - 1) * cuts + cut
+            both = gate_up(shift, 1, cut)
+            near[cut].wait_recv()
+            cs[k] = (both + pr[shift * cuts + cut].astype(F32)).astype(BF16)
+            crossing[shift, cut] = push(
+                cs.at[k], cr.at[k], c_send.at[k], c_recv.at[k], across(shift)
             )
-            across.start()
-            sends.append(across)
-    for shift in range(1, chips):
-        sends[2 * shift - 1].wait_recv()
-        own = own + cr[shift - 1].astype(F32)
-    gate = own[:cap]
-    hid[0] = (gate / (1.0 + jnp.exp(-gate)) * own[cap:]).astype(BF16)
-
-    across_h = []
-    for shift in range(1, chips):
-        copy = pltpu.make_async_remote_copy(
-            src_ref=hid.at[0],
-            dst_ref=hid.at[2 * shift],
-            send_sem=h_send.at[shift],
-            recv_sem=h_recv.at[shift],
-            device_id={"attn": side_of(shift, 1), "expert": me_e, "loop": me_l},
-            device_id_type=MESH,
-        )
-        copy.start()
-        across_h.append(copy)
-
-    def forward(shift):
-        copy = pltpu.make_async_remote_copy(
-            src_ref=hid.at[2 * shift],
-            dst_ref=hid.at[2 * shift + 1],
-            send_sem=f_send.at[shift],
-            recv_sem=f_recv.at[shift],
-            device_id=partner,
-            device_id_type=MESH,
-        )
-        copy.start()
-        return copy
+    near = to_partner(0)
+    for cut in range(cuts):
+        own[cut] = gate_up(0, 1, cut)
 
     def down(k):
         d_copies[k].wait()
         return jnp.dot(hid[k], wd[k], preferred_element_type=F32)
 
-    near = forward(0)
-    expert_out = down(0)
-    near.wait_recv()
-    expert_out = expert_out + down(1)
-    sends.append(near)
+    def spread(shift, cut):
+        k = 2 * shift * cuts + cut
+        return push(hid.at[k], hid.at[k + cuts], f_send.at[shift * cuts + cut],
+                    f_recv.at[shift * cuts + cut], partner)
+
+    expert_out = jnp.zeros((cap, part), F32)
+    far, beside = {}, {}
+    for cut in range(cuts):
+        near[cut].wait_recv()
+        both = own[cut] + pr[cut].astype(F32)
+        for shift in range(1, chips):
+            crossing[shift, cut].wait_recv()
+            both = both + cr[(shift - 1) * cuts + cut].astype(F32)
+        gate = both[:cap]
+        hid[cut] = (gate / (1.0 + jnp.exp(-gate)) * both[cap:]).astype(BF16)
+        for shift in range(1, chips):
+            k = shift * cuts + cut
+            far[shift, cut] = push(
+                hid.at[cut], hid.at[2 * shift * cuts + cut], h_send.at[k], h_recv.at[k], across(shift)
+            )
+        beside[0, cut] = spread(0, cut)
+        expert_out = expert_out + down(cut)
+    for cut in range(cuts):
+        beside[0, cut].wait_recv()
+        expert_out = expert_out + down(cuts + cut)
     for shift in range(1, chips):
-        across_h[shift - 1].wait_recv()
-        near = forward(shift)
-        expert_out = expert_out + down(2 * shift)
-        near.wait_recv()
-        expert_out = expert_out + down(2 * shift + 1)
-        sends.append(near)
+        for cut in range(cuts):
+            far[shift, cut].wait_recv()
+            beside[shift, cut] = spread(shift, cut)
+            expert_out = expert_out + down(2 * shift * cuts + cut)
+    for shift in range(1, chips):
+        for cut in range(cuts):
+            beside[shift, cut].wait_recv()
+            expert_out = expert_out + down((2 * shift + 1) * cuts + cut)
 
     if slots > cap:
         expert_out = jnp.concatenate([expert_out, jnp.zeros((slots - cap, part), F32)], axis=0)
@@ -332,23 +357,19 @@
 
     lax.fori_loop(0, tiles, pack, 0, unroll=min(8, tiles))
 
-    def send_y(d, carry):
-        to = lax.rem(me + d, total)
+    def send_y(index, lane, device):
         pltpu.make_async_remote_copy(
-            src_ref=ys.at[to],
+            src_ref=ys.at[index],
             dst_ref=yr.at[me],
             send_sem=y_send,
             recv_sem=y_recv,
-            device_id=place(to),
+            device_id=device,
             device_id_type=MESH,
         ).start()
-        return carry
-
-    lax.fori_loop(1, total, send_y, 0)
+
+    each_peer(send_y)
     yr[me] = ys[me]
     wait_all(yr, y_recv)
-    sources = total // n
-
     def add(g, sums):
         return tuple(sums[a] + yr[g * n + a].astype(F32) for a in range(n))
 
@@ -362,7 +383,7 @@
     moe = jnp.concatenate(sums, axis=1).astype(BF16).astype(F32)
     out_ref[...] = (residual + moe).astype(BF16)
 
-    for copy in sends + across_h:
+    for copy in sends:
         copy.wait_send()
     wait_all(xr, x_send)
     wait_all(yr, y_send)
@@ -392,6 +413,8 @@
     rows = here * total
     part = width // n
     quarter = gate_weight.shape[2] // n
+    cuts = CUTS if quarter % (128 * CUTS) == 0 else 1
+    piece = quarter // cuts
     slots = block_rows.shape[1] * block_rows.shape[2]
     busiest = rows // 2
     shared = -(-(2 * rows - busiest) // (experts - 1))
@@ -403,38 +426,39 @@
     scratch = [
         pltpu.VMEM((here, cache, kv_width), BF16),
         pltpu.VMEM((here, cache, kv_width), BF16),
-        pltpu.VMEM((n, part, quarter), BF16),
-        pltpu.VMEM((n, part, quarter), BF16),
-        pltpu.VMEM((n, quarter, part), BF16),
+        pltpu.VMEM((n * cuts, part, piece), BF16),
+        pltpu.VMEM((n * cuts, part, piece), BF16),
+        pltpu.VMEM((n * cuts, piece, part), BF16),
         pltpu.VMEM((n, here, part), BF16),
         pltpu.VMEM((total, here, part), BF16),
         pltpu.VMEM((rows // 8, 8, part), F32),
-        pltpu.VMEM((chips, 2 * cap, quarter), BF16),
-        pltpu.VMEM((chips, 2 * cap, quarter), BF16),
-        pltpu.VMEM((chips - 1, 2 * cap, quarter), BF16),
-        pltpu.VMEM((chips - 1, 2 * cap, quarter), BF16),
-        pltpu.VMEM((n, cap, quarter), BF16),
+        pltpu.VMEM((chips * cuts, 2 * cap, piece), BF16),
+        pltpu.VMEM((chips * cuts, 2 * cap, piece), BF16),
+        pltpu.VMEM((cuts, 2 * cap, piece), F32),
+        pltpu.VMEM(((chips - 1) * cuts, 2 * cap, piece), BF16),
+        pltpu.VMEM(((chips - 1) * cuts, 2 * cap, piece), BF16),
+        pltpu.VMEM((n * cuts, cap, piece), BF16),
         pltpu.VMEM((rows // 8, 8, part), F32),
         pltpu.VMEM((total, here, part), BF16),
         pltpu.VMEM((total, here, part), BF16),
         dma((2, here)),
-        dma((2, n)),
-        dma((n,)),
+        dma((2, n * cuts)),
+        dma((n * cuts,)),
         dma,
         dma,
-        dma((chips,)),
-        dma((chips,)),
-        dma((chips - 1,)),
-        dma((chips - 1,)),
-        dma((chips,)),
-        dma((chips,)),
-        dma((chips,)),
-        dma((chips,)),
+        dma((chips * cuts,)),
+        dma((chips * cuts,)),
+        dma(((chips - 1) * cuts,)),
+        dma(((chips - 1) * cuts,)),
+        dma((chips * cuts,)),
+        dma((chips * cuts,)),
+        dma((chips * cuts,)),
+        dma((chips * cuts,)),
         dma,
         dma,
     ]
     return pl.pallas_call(
-        functools.partial(kernel, (n, experts, loops, cap)),
+        functools.partial(kernel, (n, experts, loops, cap, cuts)),
         out_shape=jax.ShapeDtypeStruct((here, width), BF16),
         in_specs=[pl.BlockSpec(memory_space=pltpu.SMEM)] + [vmem] * 7 + [hbm] * 5,
         out_specs=vmem,

time: 32.6 us -> 32 us (0.982)
  Pallas kernels: 31 us -> 30.4 us
    pallas_call x1, Pallas kernels: 31 us -> 30.4 us  [per_device(): pl.pallas_call(functools.partial(kernel, (n, experts, loops, cap, cuts)),...]
where the time goes in v2:
time: 32 us; the launch traced here: 31.8 us
  Pallas kernels  30.4 us (95%)
  local copies, waits for them, and re-layouts  1.32 us (4%)
    pallas_call x1, Pallas kernels, per_device(): pl.pallas_call(functools.partial(kernel, (n, experts, loops, cap, cuts)),...  30.4 us
    unnamed x1, local copies, waits for them, and re-layouts  1.32 us

profile of v2, /device:TPU:0, one launch (start us, length us, event | category | flops | bytes accessed | tf_op | source)
XLA Modules:
  0.0 31.8 jit_solution(3386277644683219071)
XLA Ops:
  0.0 30.4 %moe_decode.1 = bf16[2,3072]{1,0:T(2,128)(2,1)} custom-call(s32[2]{0:T(128)} %len_ref.1, bf16[2,3072]{1,0:T(2,128)(2,1)} %resid_ref.1, bf16[2,3072]{1,0:T(2,128)(2,1)} %query_ref.1, bf16[2,512]{1,0:T(2,128)(2,1)} %nk_ref.1, bf16[2,512]{1,0:T(2,128)(2,1)} %nv_ref.1, f32[1,3072]{1,0:T(1,128)} %bitcast.3, s32[1,128]{1,0:T(1,128)} %bitcast.4, f32[1,128]{1,0:T(1,128)} %bitcast.5, ...), custom_call_target="tpu_custom_call" | custom-call | tf_op jit(solution)/shard_map/moe_decode/pallas_call | solution.py:460
  30.5 1.3 %copy.15 = bf16[2,3072]{1,0:T(2,128)(2,1)} copy(bf16[2,3072]{1,0:T(2,128)(2,1)} %moe_decode.1) | data formatting | bytes 24576
